TPU v7x, 256 devices: a whole 4x4x8 slice. The times are simulated.
256 devices in a mesh: circ: 64 (over z, y_hi, x), ax: 4 (over y_lo, core).
Axes of the slice: x: 4, y: 4 (y_hi: 2, y_lo: 2; y = y_hi * 2 + y_lo), z: 8, core: 2. Of those that a mesh axis runs over, the one named last changes fastest.
Arguments:
- fields: float32 [3, 8, 512, 1024], P(None, None, 'circ', 'ax'), may hold values from -6 to 6
Outputs:
- deriv_circ: float32 [3, 8, 512, 1024], P(None, None, 'circ', 'ax')
- deriv_axial: float32 [3, 8, 512, 1024], P(None, None, 'circ', 'ax')
- filtered: float32 [3, 8, 512, 1024], P(None, None, 'circ', 'ax')
All inputs are finite; a program needn't handle non-finite values.
Results may differ from a plain program's by a relative error of at most 0.0003.
Values sent between devices are 32-bit elements; how exact they have to be, the bound alone decides.
No kernel may reach another device: no remote copies, remote signals or barrier semaphores. Data moves between devices by JAX's collectives and lax.ppermute only.
A program may use at most 64 MiB of HBM per device.

v0:
```python
import math
import jax
import jax.numpy as jnp
import numpy as np
from jax import lax
from jax.sharding import PartitionSpec as P

DERIV_NEAR = 14.0 / 9.0
DERIV_FAR = 1.0 / 9.0
ALPHA_DERIV = 1.0 / 3.0
ALPHA_FILTER = 0.4999
PRECISE = lax.Precision.HIGHEST


def with_halo(value, sides, width, wrap):
    for axis, dim in sides:
        peers, length = (lax.axis_size(axis), value.shape[dim])
        up = [(i, (i + 1) % peers) for i in range(peers if wrap else peers - 1)]
        down = [(j, i) for i, j in up]
        last = lax.slice_in_dim(value, length - width, length, axis=dim)
        initial = lax.slice_in_dim(value, 0, width, axis=dim)
        before = lax.ppermute(last, axis, up)
        after = lax.ppermute(initial, axis, down)
        value = jnp.concatenate([before, value, after], axis=dim)
    return value


def entering_2(part, axis, combine, identity, reverse):
    count = lax.axis_size(axis)
    place = lax.axis_index(axis)
    ahead = count - 1 - place if reverse else place
    gathered = jax.tree.map(lambda a: lax.all_gather(a, axis), part)
    state = jax.tree.map(lambda a, e: jnp.zeros_like(a) + jnp.asarray(e, a.dtype), part, identity)

    def one(step, state):
        source = count - 1 - step if reverse else step
        return combine(
            state, jax.tree.map(lambda a: lax.dynamic_index_in_dim(a, source, 0, False), gathered)
        )

    return lax.fori_loop(0, ahead, one, state)


def filter_terms(coupling):
    return [
        (193.0 + 126.0 * coupling) / 256.0,
        (105.0 + 302.0 * coupling) / 256.0,
        15.0 * (2.0 * coupling - 1.0) / 64.0,
        45.0 * (1.0 - 2.0 * coupling) / 512.0,
        5.0 * (2.0 * coupling - 1.0) / 256.0,
        (1.0 - 2.0 * coupling) / 512.0,
    ]


def root_of(coupling):
    return (-1.0 + math.sqrt(1.0 - 4.0 * coupling * coupling)) / (2.0 * coupling)


def signed_power(exponent, log_sizes):
    magnitude = jnp.exp(exponent[..., None].astype(jnp.float32) * log_sizes)
    parity = (exponent % 2).astype(jnp.float32)
    return magnitude * (1.0 - 2.0 * parity)[..., None]


def affine_chain(earlier, later):
    return (earlier[0] * later[0], later[0] * earlier[1] + later[1])


def running_products(values):
    result = np.zeros(len(values))
    running = 1.0
    for place in range(len(values)):
        running = running * values[place]
        result[place] = running
    return result


def axial_rhs(shifted, row_index, line_length):
    interior = 0.5 * DERIV_NEAR * (shifted(1) - shifted(-1)) + 0.25 * DERIV_FAR * (
        shifted(2) - shifted(-2)
    )
    row_opening = -2.5 * shifted(0) + 2.0 * shifted(1) + 0.5 * shifted(2)
    row_second = 0.75 * (shifted(1) - shifted(-1))
    row_closing = 2.5 * shifted(0) - 2.0 * shifted(-1) - 0.5 * shifted(-2)
    result = jnp.where(row_index == 0, row_opening, interior)
    result = jnp.where((row_index == 1) | (row_index == line_length - 2), row_second, result)
    return jnp.where(row_index == line_length - 1, row_closing, result)


def bands_table(line_length):
    band_lower = np.full(line_length, ALPHA_DERIV)
    band_lower[0] = 0.0
    band_lower[1] = 0.25
    band_lower[line_length - 2] = 0.25
    band_lower[line_length - 1] = 2.0
    band_middle = np.ones(line_length)
    band_upper = np.full(line_length, ALPHA_DERIV)
    band_upper[0] = 2.0
    band_upper[1] = 0.25
    band_upper[line_length - 2] = 0.25
    band_upper[line_length - 1] = 0.0
    return (band_lower, band_middle, band_upper)


def thomas_tables(line_cells, axial_count):
    line_length = line_cells * axial_count
    band_lower, band_middle, band_upper = bands_table(line_length)
    pivots = np.zeros(line_length)
    factors = np.zeros(line_length)
    pivots[0] = band_middle[0]
    for row_number in range(1, line_length):
        factors[row_number] = -band_lower[row_number] / pivots[row_number - 1]
        pivots[row_number] = (
            band_middle[row_number] + factors[row_number] * band_upper[row_number - 1]
        )
    backs = -band_upper / pivots
    fwd_blocks, fwd_grows, back_blocks, back_grows, inv_pivots = ([], [], [], [], [])
    for place in range(axial_count):
        base_row = place * line_cells
        seg_fwd = factors[base_row : base_row + line_cells]
        seg_back = backs[base_row : base_row + line_cells]
        block_fwd = np.zeros((line_cells, line_cells))
        block_back = np.zeros((line_cells, line_cells))
        for target in range(line_cells):
            running = 1.0
            block_fwd[target, target] = 1.0
            for source in range(target - 1, -1, -1):
                running = running * seg_fwd[source + 1]
                block_fwd[target, source] = running
            running = 1.0
            block_back[target, target] = 1.0
            for source in range(target + 1, line_cells):
                running = running * seg_back[source - 1]
                block_back[target, source] = running
        fwd_blocks.append(block_fwd)
        fwd_grows.append(running_products(seg_fwd))
        back_blocks.append(block_back)
        back_grows.append(running_products(seg_back[::-1])[::-1])
        inv_pivots.append(1.0 / pivots[base_row : base_row + line_cells])
    return [
        jnp.asarray(np.stack(table), jnp.float32)
        for table in (fwd_blocks, fwd_grows, back_blocks, back_grows, inv_pivots)
    ]


def shards(fields):
    cells = fields.shape[2]
    line_cells = fields.shape[3]
    roots = [root_of(ALPHA_DERIV), root_of(ALPHA_FILTER)]
    circ_count = lax.axis_size("circ")
    circ_place = lax.axis_index("circ")
    loop_cells = cells * circ_count
    log_sizes = jnp.asarray([math.log(abs(root_value)) for root_value in roots], jnp.float32)
    wrap_scale = jnp.asarray(
        [1.0 / (1.0 - root_value**loop_cells) for root_value in roots], jnp.float32
    )
    padded = with_halo(fields, (("circ", 2),), 5, True)

    def circ_take(offset):
        return padded[:, :, 5 + offset : 5 + offset + cells, :]

    circ_right = 0.5 * DERIV_NEAR * (circ_take(1) - circ_take(-1)) + 0.25 * DERIV_FAR * (
        circ_take(2) - circ_take(-2)
    )
    terms = filter_terms(ALPHA_FILTER)
    filter_right = terms[0] * circ_take(0)
    for offset in range(1, 6):
        filter_right = filter_right + 0.5 * terms[offset] * (circ_take(offset) + circ_take(-offset))
    scaled = jnp.stack([circ_right * (1.0 + roots[0] ** 2), filter_right * (1.0 + roots[1] ** 2)])
    cell_steps = np.arange(cells)
    cell_gap = cell_steps[:, None] - cell_steps[None, :]
    forward_np = np.stack(
        [
            np.where(cell_gap >= 0, root_value ** np.maximum(cell_gap, 0), 0.0)
            for root_value in roots
        ]
    )
    backward_np = np.stack(
        [
            np.where(cell_gap <= 0, root_value ** np.maximum(-cell_gap, 0), 0.0)
            for root_value in roots
        ]
    )
    forward_table = jnp.asarray(forward_np, jnp.float32)
    backward_table = jnp.asarray(backward_np, jnp.float32)
    grow_forward = jnp.asarray(
        np.stack([root_value ** (cell_steps + 1) for root_value in roots]), jnp.float32
    )
    grow_backward = jnp.asarray(
        np.stack([root_value ** (cells - cell_steps) for root_value in roots]), jnp.float32
    )

    def circ_carry(state, backward):
        piece = lax.all_gather(state[None], "circ", axis=0, tiled=True)
        shard_ids = jnp.arange(piece.shape[0], dtype=jnp.int32)
        if backward:
            distance = (shard_ids - circ_place - 1) % circ_count
        else:
            distance = (circ_place - shard_ids - 1) % circ_count
        weights = signed_power(distance * cells, log_sizes) * wrap_scale
        return jnp.zeros_like(state) + jnp.einsum(
            "qs,qsfna->sfna", weights, piece, precision=PRECISE
        )

    partial_forward = jnp.einsum("sjk,sfnka->sfnja", forward_table, scaled, precision=PRECISE)
    incoming = circ_carry(partial_forward[:, :, :, -1, :], False)
    forward_full = (
        partial_forward + grow_forward[:, None, None, :, None] * incoming[:, :, :, None, :]
    )
    partial_back = jnp.einsum("sjk,sfnka->sfnja", backward_table, forward_full, precision=PRECISE)
    incoming_back = circ_carry(partial_back[:, :, :, 0, :], True)
    solved = partial_back + grow_backward[:, None, None, :, None] * incoming_back[:, :, :, None, :]
    deriv_circ = solved[0]
    filtered = solved[1]
    axial_count = lax.axis_size("ax")
    axial_place = lax.axis_index("ax")
    line_length = line_cells * axial_count
    padded_axial = with_halo(fields, (("ax", 3),), 2, False)

    def axial_take(offset):
        return padded_axial[:, :, :, 2 + offset : 2 + offset + line_cells]

    global_rows = axial_place * line_cells + jnp.arange(line_cells, dtype=jnp.int32)
    axial_right = axial_rhs(axial_take, global_rows, line_length)
    tables = thomas_tables(line_cells, axial_count)
    fwd_block, fwd_grow, back_block, back_grow, inv_pivot = [
        lax.dynamic_index_in_dim(table, axial_place, 0, keepdims=False) for table in tables
    ]

    def axial_carry(multiplier, state, backward):
        identity = (jnp.ones_like(multiplier), jnp.zeros_like(state))
        return entering_2((multiplier, state), "ax", affine_chain, identity, backward)[1]

    local_fwd = jnp.einsum("fnck,jk->fncj", axial_right, fwd_block, precision=PRECISE)
    entering = axial_carry(fwd_grow[-1].reshape(1, 1, 1), local_fwd[:, :, :, -1], False)
    eliminated = (local_fwd + fwd_grow * entering[:, :, :, None]) * inv_pivot
    local_back = jnp.einsum("fnck,jk->fncj", eliminated, back_block, precision=PRECISE)
    entering_back = axial_carry(back_grow[0].reshape(1, 1, 1), local_back[:, :, :, 0], True)
    deriv_axial = local_back + back_grow * entering_back[:, :, :, None]
    return (deriv_circ, deriv_axial, filtered)


def solution(mesh):
    placed = (P(None, None, "circ", "ax"),)
    return jax.shard_map(
        shards,
        mesh=mesh,
        in_specs=placed,
        out_specs=(
            P(None, None, "circ", "ax"),
            P(None, None, "circ", "ax"),
            P(None, None, "circ", "ax"),
        ),
        check_vma=False,
    )
```

profile of v0, /device:TPU:2, one launch (start us, length us, event | category | flops | bytes accessed | tf_op | source)
XLA Modules:
  0.0 288.8 jit_solution(12185485005442516595)
XLA Ops:
  7.2 0.0 copy-start.2
  7.2 0.0 copy-start.6
  7.2 0.0 all-gather.9.cloned.1.call-start
  7.2 1.1 fusion.99
  8.3 2.3 collective-permute-start
  10.6 0.9 constant_dynamic-update-slice_fusion.1
  11.6 3.5 %collective-permute-done = f32[3,8,5,256]{3,2,1,0:T(8,128)S(1)} collective-permute-done((f32[3,8,5,256]{3,2,1,0:T(8,128)S(1)}, f32[3,8,5,256]{3,2,1,0:T(8,128)S(1)}, u32[]{:S(2)}, u32[]{:S(2)}) %collective-permute-start) | collective-permute-done | bytes 122912 | tf_op jit(solution)/shard_map/ppermute | solution.py:23
  15.1 9.1 %collective-permute-done.1 = f32[3,8,5,256]{3,2,1,0:T(8,128)S(1)} collective-permute-done((f32[3,8,5,256]{3,2,1,0:T(8,128)S(1)}, f32[3,8,5,256]{3,2,1,0:T(8,128)S(1)}, u32[]{:S(2)}, u32[]{:S(2)}) %collective-permute-start.1) | collective-permute-done | bytes 122912 | tf_op jit(solution)/shard_map/ppermute | solution.py:22
  24.2 2.5 multiply_bitcast_fusion
  26.8 0.5 convolution_bitcast_fusion.1
  27.3 0.6 copy.19
  27.9 0.0 all-gather.9.cloned.1.call-update
  27.9 0.0 all-gather.11.cloned.1.call-start
  28.1 0.1 multiply_multiply_fusion
  28.1 121.8 %all-gather.9.cloned.1.call-done = f32[128,3,8,1,256]{4,2,3,1,0:T(8,128)} async-done(((f32[2,3,8,1,256]{4,2,3,1,0:T(8,128)}), f32[128,3,8,1,256]{4,2,3,1,0:T(8,128)}) %all-gather.9.cloned.1.call-update) | async-done | bytes 3145744 | tf_op jit(solution)/shard_map/all_gather | solution.py:194
  150.0 5.1 %fusion.2 = f32[2,1,3,8,256]{4,1,3,2,0:T(1,128)S(1)} fusion(f32[64,2,1,1,1]{0,2,4,3,1:T(1,128)S(1)} %bitcast.83, f32[64,2,3,8,256]{4,3,2,1,0:T(8,128)} %bitcast.77), kind=kOutput, calls=%fused_computation.6 | convolution fusion | flops 9437184 | bytes 3195392 | tf_op jit(solution)/shard_map/qs,qsfna->sfna/dot_general | solution.py:201
  155.1 0.5 convolution_bitcast_fusion
  155.7 0.6 copy.20
  156.3 0.0 all-gather.11.cloned.1.call-update
  156.3 0.1 fusion.98
  156.4 1.3 collective-permute-start.3
  157.7 3.0 %collective-permute-start.2 = (f32[3,8,8,2]{3,2,1,0:T(8,128)S(1)}, f32[3,8,8,2]{3,2,1,0:T(8,128)S(1)}, u32[]{:S(2)}, u32[]{:S(2)}) collective-permute-start(f32[3,8,8,2]{3,2,1,0:T(8,128)S(1)} %get-tuple-element.159), channel_id=1, source_target_pairs={{0,1},{1,2},{2,3},{4,5},{5,6},{6,7},{8,9},{9,10},{10,11},{12,13},{... | collective-permute-start | bytes 4616 | tf_op jit(solution)/shard_map/ppermute | solution.py:22
  160.8 0.6 dynamic-slice
  161.4 1.3 dynamic-slice.2
  162.7 1.3 bitcast_dynamic-update-slice_fusion.1
  164.0 1.4 bitcast_dynamic-update-slice_fusion
  165.4 0.7 constant_dynamic-slice_fusion.5
  166.1 0.7 constant_dynamic-slice_fusion.3
  166.8 6.3 %all-reduce.2 = (f32[4]{0:T(128)S(1)}, f32[4]{0:T(128)S(1)}) all-reduce(f32[4]{0:T(128)S(1)} %bitcast_dynamic-update-slice_fusion.1, f32[4]{0:T(128)S(1)} %bitcast_dynamic-update-slice_fusion), channel_id=4, replica_groups=mesh['circ'=64,'ax'=4] {'ax'}, use_global_device_ids=true, to_apply=%add | all-reduce | flops 8 | bytes 64
  173.1 1.5 fusion.11
  174.7 0.1 slice.150
  174.8 0.2 copy.21
  175.0 5.2 %all-gather.3 = f32[12,8,8,1]{2,1,3,0:T(8,128)S(1)} all-gather(f32[3,8,8,1]{2,1,3,0:T(8,128)S(1)} %copy.21), channel_id=5, replica_groups=mesh['circ'=64,'ax'=4] {'ax'}, dimensions={0}, use_global_device_ids=true | all-gather | bytes 3840 | tf_op jit(solution)/shard_map/all_gather | solution.py:32
  180.2 1.4 fusion.9
  181.6 0.2 copy.22
  181.8 8.7 %all-gather.5 = f32[12,8,8,1]{2,1,3,0:T(8,128)S(1)} all-gather(f32[3,8,8,1]{2,1,3,0:T(8,128)S(1)} %copy.22), channel_id=7, replica_groups=mesh['circ'=64,'ax'=4] {'ax'}, dimensions={0}, use_global_device_ids=true | all-gather | bytes 3840 | tf_op jit(solution)/shard_map/all_gather | solution.py:32
  190.5 4.0 %while.27 = (s32[]{:T(128)}, f32[3,8,8]{2,1,0:T(8,128)S(1)}, s32[]{:T(128)}, f32[4,1,1,1]{0,3,2,1:T(1,128)S(1)}, f32[4,3,8,8]{3,2,1,0:T(8,128)S(1)}, /*index=5*/s32[]{:T(128)}, s32[]{:T(128)}, s32[]{:T(128)}, s32[]{:T(128)}) while((s32[]{:T(128)}, f32[3,8,8]{2,1,0:T(8,128)S(1)}, s32[]{:T(128)}, f32[4,1,1,1]{0,3,2,1:T(1,128)S(1)}, ...), condition=%wide.region_3.4_spmd, body=%wide.region_2.3_spmd.sunk | while | flops 390 | bytes 2463 | solution.py:41
  190.5 0.6 constant_dynamic-slice_fusion.9
  191.1 0.7 bitcast_add_fusion.5
  191.8 0.6 constant_dynamic-slice_fusion.9
  192.4 0.7 bitcast_add_fusion.5
  193.1 0.6 constant_dynamic-slice_fusion.9
  193.7 0.7 bitcast_add_fusion.5
  194.5 0.8 multiply_add_fusion.1
  195.3 80.7 %all-gather.11.cloned.1.call-done = f32[128,3,8,1,256]{4,2,3,1,0:T(8,128)} async-done(((f32[2,3,8,1,256]{4,2,3,1,0:T(8,128)}), f32[128,3,8,1,256]{4,2,3,1,0:T(8,128)}) %all-gather.11.cloned.1.call-update) | async-done | bytes 3145744 | tf_op jit(solution)/shard_map/all_gather | solution.py:194
  276.0 5.1 %fusion = f32[2,1,3,8,256]{4,1,3,2,0:T(1,128)S(1)} fusion(f32[64,2,1,1,1]{0,2,4,3,1:T(1,128)S(1)} %bitcast.82, f32[64,2,3,8,256]{4,3,2,1,0:T(8,128)} %bitcast.76), kind=kOutput, calls=%fused_computation.4 | convolution fusion | flops 9437184 | bytes 3195392 | tf_op jit(solution)/shard_map/qs,qsfna->sfna/dot_general | solution.py:201
  281.1 0.1 multiply_add_fusion
  281.2 0.8 slice_bitcast_fusion
  (33 shorter events, 0.2 us)
Async XLA Ops:
  7.2 19.6 %copy-start.2 = (f32[2,8,8,1,1]{2,1,4,3,0:T(8,128)S(1)}, f32[2,8,8,1,1]{2,1,4,3,0:T(8,128)}, u32[]{:S(2)}) copy-start(f32[2,8,8,1,1]{2,1,4,3,0:T(8,128)} %constant.206) | copy-start | bytes 1540
  7.2 20.9 %copy-start.5 = (f32[2]{0:T(128)S(1)}, f32[2]{0:T(128)}, u32[]{:S(2)}) copy-start(f32[2]{0:T(128)} %constant.182.clone) | copy-start | bytes 28
  7.2 20.9 %copy-start.6 = (f32[2]{0:T(128)S(1)}, f32[2]{0:T(128)}, u32[]{:S(2)}) copy-start(f32[2]{0:T(128)} %constant.183.clone) | copy-start | bytes 28
  7.2 142.8 %all-gather.9.cloned.1.call-start = ((), (), s32[]{:S(2)}) async-start(), calls=%async_computation | async-start | bytes 3194880 | tf_op jit(solution)/shard_map/all_gather | solution.py:194
  8.3 6.7 %collective-permute-start = (f32[3,8,5,256]{3,2,1,0:T(8,128)S(1)}, f32[3,8,5,256]{3,2,1,0:T(8,128)S(1)}, u32[]{:S(2)}, u32[]{:S(2)}) collective-permute-start(f32[3,8,5,256]{3,2,1,0:T(8,128)S(1)} %get-tuple-element.162), channel_id=1, source_target_pairs={{4,0},{8,4},{12,8},{16,12},{20,16},{24,20},{28,24},{32,28},{36,32}... | collective-permute-start | bytes 368648 | tf_op jit(solution)/shard_map/ppermute | solution.py:23
  10.6 13.6 %collective-permute-start.1 = (f32[3,8,5,256]{3,2,1,0:T(8,128)S(1)}, f32[3,8,5,256]{3,2,1,0:T(8,128)S(1)}, u32[]{:S(2)}, u32[]{:S(2)}) collective-permute-start(f32[3,8,5,256]{3,2,1,0:T(8,128)S(1)} %get-tuple-element.163), channel_id=1, source_target_pairs={{0,4},{4,8},{8,12},{12,16},{16,20},{20,24},{24,28},{28,32},{32,36}... | collective-permute-start | bytes 368648 | tf_op jit(solution)/shard_map/ppermute | solution.py:22
  15.0 140.1 %copy-start.1 = (f32[2,8,8,1,1]{2,1,4,3,0:T(8,128)S(1)}, f32[2,8,8,1,1]{2,1,4,3,0:T(8,128)}, u32[]{:S(2)}) copy-start(f32[2,8,8,1,1]{2,1,4,3,0:T(8,128)} %constant.207) | copy-start | bytes 1540
  15.1 140.0 %copy-start.4 = (f32[2,8]{1,0:T(2,128)S(1)}, f32[2,8]{1,0:T(2,128)}, u32[]{:S(2)}) copy-start(f32[2,8]{1,0:T(2,128)} %constant.186.clone) | copy-start | bytes 196
  26.8 129.6 %copy-start = (f32[3,8,8,256]{3,2,1,0:T(8,128)S(1)}, f32[3,8,8,256]{3,2,1,0:T(8,128)}, u32[]{:S(2)}) copy-start(f32[3,8,8,256]{3,2,1,0:T(8,128)} %param.16) | copy-start | bytes 589828
  26.8 134.0 %copy-start.7 = (u32[256]{0:T(256)S(1)}, u32[256]{0:T(256)}, u32[]{:S(2)}) copy-start(u32[256]{0:T(256)} %constant.196) | copy-start | bytes 3076
  27.9 248.0 %all-gather.11.cloned.1.call-start = ((), (), s32[]{:S(2)}) async-start(), calls=%async_computation.1 | async-start | bytes 3194880 | tf_op jit(solution)/shard_map/all_gather | solution.py:194
  156.4 16.7 %collective-permute-start.3 = (f32[3,8,8,2]{3,2,1,0:T(8,128)S(1)}, f32[3,8,8,2]{3,2,1,0:T(8,128)S(1)}, u32[]{:S(2)}, u32[]{:S(2)}) collective-permute-start(f32[3,8,8,2]{3,2,1,0:T(8,128)S(1)} %get-tuple-element.160), channel_id=1, source_target_pairs={{1,0},{2,1},{3,2},{5,4},{6,5},{7,6},{9,8},{10,9},{11,10},{13,12},{... | collective-permute-start | bytes 4616 | tf_op jit(solution)/shard_map/ppermute | solution.py:23
  157.7 15.4 %collective-permute-start.2 = (f32[3,8,8,2]{3,2,1,0:T(8,128)S(1)}, f32[3,8,8,2]{3,2,1,0:T(8,128)S(1)}, u32[]{:S(2)}, u32[]{:S(2)}) collective-permute-start(f32[3,8,8,2]{3,2,1,0:T(8,128)S(1)} %get-tuple-element.159), channel_id=1, source_target_pairs={{0,1},{1,2},{2,3},{4,5},{5,6},{6,7},{8,9},{9,10},{10,11},{12,13},{... | collective-permute-start | bytes 4616 | tf_op jit(solution)/shard_map/ppermute | solution.py:22
  174.7 106.4 %copy-start.3 = (f32[2,8]{1,0:T(2,128)S(1)}, f32[2,8]{1,0:T(2,128)}, u32[]{:S(2)}) copy-start(f32[2,8]{1,0:T(2,128)} %constant.187.clone) | copy-start | bytes 196
Sparse Core Ops, SparseCore 0:
  28.1 121.8 all-gather.8
  156.5 119.4 all-gather.10
where the time goes:
time: 289 us
  waiting for transfers between devices  215 us (74%)
  blocking collectives  20.2 us (7%)
  between operations  14.4 us (5%)
  matrix products  14.1 us (5%)
  local copies, waits for them, and re-layouts  12.5 us (4%)
  starting transfers between devices  6.73 us (2%)
  other arithmetic  5.5 us (2%)
    all_gather x2, waiting for transfers between devices, circ_carry(): piece = lax.all_gather(state[None], 'circ', axis=0, tiled=True)  203 us
    all_gather x2, blocking collectives, entering_2(): gathered = jax.tree.map(lambda a: lax.all_gather(a, axis), part)  13.9 us
    dot_general x2, matrix products, circ_carry(): jnp.einsum('qs,qsfna->sfna', weights, piece, precision=PRECISE)  10.2 us
    ppermute x2, waiting for transfers between devices, with_halo(): before = lax.ppermute(last, axis, up)  9.15 us
    unnamed x1, blocking collectives  6.26 us
  transfers between devices with their start and end apart: 6, of which 4 were waited for; matrix products, arithmetic and copies ran while one was open for 5% of the time, Pallas kernels for 0%

commit v1 on v0

--- a/solution.py
+++ b/solution.py
@@ -4,12 +4,19 @@
 import numpy as np
 from jax import lax
 from jax.sharding import PartitionSpec as P
+from jax.lax import all_to_all, axis_size
 
 DERIV_NEAR = 14.0 / 9.0
 DERIV_FAR = 1.0 / 9.0
 ALPHA_DERIV = 1.0 / 3.0
 ALPHA_FILTER = 0.4999
 PRECISE = lax.Precision.HIGHEST
+
+
+def lines_pass(lane_axis, sheet):
+    return jnp.concatenate(
+        all_to_all(jnp.stack(axis_size(lane_axis) * [sheet]), lane_axis, 0, 0), axis=0
+    )
 
 
 def with_halo(value, sides, width, wrap):
@@ -191,7 +198,7 @@
     )
 
     def circ_carry(state, backward):
-        piece = lax.all_gather(state[None], "circ", axis=0, tiled=True)
+        piece = lines_pass("circ", state[None])
         shard_ids = jnp.arange(piece.shape[0], dtype=jnp.int32)
         if backward:
             distance = (shard_ids - circ_place - 1) % circ_count

time: 289 us -> 200 us (0.69)
  waiting for transfers between devices: 215 us -> 96.4 us
  starting transfers between devices: 6.73 us -> 25.2 us
  between operations: 14.4 us -> 0.86 us
  local copies, waits for them, and re-layouts: 12.5 us -> 25.9 us
  blocking collectives: 20.2 us -> 27.4 us
  other arithmetic: 5.5 us -> 11 us
    all_gather x2 -> x0, waiting for transfers between devices: 203 us -> none  [circ_carry(): piece = lax.all_gather(state[None], 'circ', axis=0, tiled=True)]
    all_to_all x0 -> x2, waiting for transfers between devices: none -> 83.7 us  [lines_pass(): all_to_all(jnp.stack(axis_size(lane_axis) * [sheet]), lane_axis, 0, 0)]
    all_to_all x0 -> x2, starting transfers between devices: none -> 19.7 us  [lines_pass(): all_to_all(jnp.stack(axis_size(lane_axis) * [sheet]), lane_axis, 0, 0)]
    all_gather x2, blocking collectives: 13.9 us -> 19.1 us  [entering_2(): gathered = jax.tree.map(lambda a: lax.all_gather(a, axis), part)]
    another operation x2 -> x4, local copies, waits for them, and re-layouts: 0.01 us -> 4.05 us  [the longest x2 4.05 us: lines_pass(): jnp.stack(axis_size(lane_axis) * [sheet])]
    dot_general x2, matrix products: 10.2 us -> 6.57 us  [circ_carry(): jnp.einsum('qs,qsfna->sfna', weights, piece, precision=PRECISE)]
  transfers between devices with their start and end apart: 6 -> 6, of which waited for: 4 -> 4; matrix products, arithmetic and copies ran while one was open for 5% -> 15% of each run, Pallas kernels for 0% -> 0%
where the time goes in v1:
time: 200 us; the launch traced here: 199 us
  waiting for transfers between devices  96.4 us (48%)
  blocking collectives  27.4 us (14%)
  local copies, waits for them, and re-layouts  25.9 us (13%)
  starting transfers between devices  25.2 us (13%)
  matrix products  12.2 us (6%)
  other arithmetic  11 us (6%)
    all_to_all x2, waiting for transfers between devices, lines_pass(): all_to_all(jnp.stack(axis_size(lane_axis) * [sheet]), lane_axis, 0, 0)  83.7 us
    all_to_all x2, starting transfers between devices, lines_pass(): all_to_all(jnp.stack(axis_size(lane_axis) * [sheet]), lane_axis, 0, 0)  19.7 us
    all_gather x2, blocking collectives, entering_2(): gathered = jax.tree.map(lambda a: lax.all_gather(a, axis), part)  19.1 us
    ppermute x2, waiting for transfers between devices, with_halo(): before = lax.ppermute(last, axis, up)  9.18 us
    unnamed x1, blocking collectives  8.29 us
    unnamed x22, local copies, waits for them, and re-layouts  6.61 us
    dot_general x2, matrix products, circ_carry(): jnp.einsum('qs,qsfna->sfna', weights, piece, precision=PRECISE)  6.57 us
    add x3, other arithmetic, affine_chain(): return (earlier[0] * later[0], later[0] * earlier[1] + later[1])  4.07 us
  transfers between devices with their start and end apart: 6, of which 4 were waited for; matrix products, arithmetic and copies ran while one was open for 15% of the time, Pallas kernels for 0%

profile of v1, /device:TPU:2, one launch (start us, length us, event | category | flops | bytes accessed | tf_op | source)
XLA Modules:
  0.0 198.9 jit_solution(6882027297634672441)
XLA Ops:
  0.6 1.1 fusion.99
  1.7 2.3 %collective-permute-start = (f32[3,8,5,256]{3,2,1,0:T(8,128)S(1)}, f32[3,8,5,256]{3,2,1,0:T(8,128)S(1)}, u32[]{:S(2)}, u32[]{:S(2)}) collective-permute-start(f32[3,8,5,256]{3,2,1,0:T(8,128)S(1)} %get-tuple-element.162), channel_id=1, source_target_pairs={{4,0},{8,4},{12,8},{16,12},{20,16},{24,20},{28,24},{32,28},{36,32}... | collective-permute-start | bytes 368648 | tf_op jit(solution)/shard_map/ppermute | solution.py:30
  4.0 0.9 constant_dynamic-update-slice_fusion.1
  5.0 3.4 %collective-permute-done = f32[3,8,5,256]{3,2,1,0:T(8,128)S(1)} collective-permute-done((f32[3,8,5,256]{3,2,1,0:T(8,128)S(1)}, f32[3,8,5,256]{3,2,1,0:T(8,128)S(1)}, u32[]{:S(2)}, u32[]{:S(2)}) %collective-permute-start) | collective-permute-done | bytes 122912 | tf_op jit(solution)/shard_map/ppermute | solution.py:30
  8.4 9.2 %collective-permute-done.1 = f32[3,8,5,256]{3,2,1,0:T(8,128)S(1)} collective-permute-done((f32[3,8,5,256]{3,2,1,0:T(8,128)S(1)}, f32[3,8,5,256]{3,2,1,0:T(8,128)S(1)}, u32[]{:S(2)}, u32[]{:S(2)}) %collective-permute-start.1) | collective-permute-done | bytes 122912 | tf_op jit(solution)/shard_map/ppermute | solution.py:29
  17.6 3.1 %multiply_bitcast_fusion = (f32[1,3,8,8,256]{4,3,2,1,0:T(8,128)S(1)}, f32[1,3,8,8,256]{4,3,2,1,0:T(8,128)S(1)}, f32[3,8,8,258]{3,2,1,0:T(8,128)}) fusion(f32[3,8,13,256]{3,2,1,0:T(8,128)S(1)} %constant_dynamic-update-slice_fusion, f32[3,8,8,256]{3,2,1,0:T(8,128)} %param.16, f32[3,8,5,256]{3,2,1,0:T(8,128)S(1)} %collective-permute-done.1), kind=kLoop, calls=%fused_computation.79 | loop fusion | flops 1474559 | bytes 1892352 | tf_op jit(solution)/shard_map/stack | solution.py:176
  21.3 2.0 %stack.18 = f32[64,1,2,3,8,256]{5,4,3,2,1,0:T(8,128)} broadcast(f32[2,3,8,256]{3,2,1,0:T(8,128)S(1)} %bitcast.88), dimensions={2,3,4,5} | broadcast | bytes 3194880 | tf_op jit(solution)/shard_map/stack | solution.py:18
  23.3 11.6 %all-to-all-start = ((f32[64,1,2,3,8,256]{5,4,3,2,1,0:T(8,128)}), f32[64,1,2,3,8,256]{5,4,3,2,1,0:T(8,128)S(1)}, u32[]{:S(2)}, u32[]{:S(2)}) async-start(f32[64,1,2,3,8,256]{5,4,3,2,1,0:T(8,128)} %stack.18), calls=%async_computation | async-start | bytes 6291456 | tf_op jit(solution)/shard_map/all_to_all | solution.py:18
  35.0 0.8 multiply_multiply_fusion
  35.8 71.7 %all-to-all-done = f32[64,1,2,3,8,256]{5,4,3,2,1,0:T(8,128)S(1)} async-done(((f32[64,1,2,3,8,256]{5,4,3,2,1,0:T(8,128)}), f32[64,1,2,3,8,256]{5,4,3,2,1,0:T(8,128)S(1)}, u32[]{:S(2)}, u32[]{:S(2)}) %all-to-all-start) | async-done | bytes 3145760 | tf_op jit(solution)/shard_map/all_to_all | solution.py:18
  107.5 3.3 %fusion.2 = f32[2,1,3,8,256]{4,1,3,2,0:T(1,128)S(1)} fusion(f32[64,2,1,1,1]{0,2,4,3,1:T(1,128)S(1)} %bitcast.91, f32[64,2,3,8,256]{4,3,2,1,0:T(8,128)S(1)} %bitcast.83), kind=kOutput, calls=%fused_computation.6 | convolution fusion | flops 9437184 | bytes 3195392 | tf_op jit(solution)/shard_map/qs,qsfna->sfna/dot_general | solution.py:208
  110.8 1.2 convolution_bitcast_fusion
  112.1 2.0 %stack.19 = f32[64,1,2,3,8,256]{5,4,3,2,1,0:T(8,128)} broadcast(f32[2,3,8,256]{3,2,1,0:T(8,128)S(1)} %bitcast.89), dimensions={2,3,4,5} | broadcast | bytes 3194880 | tf_op jit(solution)/shard_map/stack | solution.py:18
  114.1 8.1 %all-to-all-start.1 = ((f32[64,1,2,3,8,256]{5,4,3,2,1,0:T(8,128)}), f32[64,1,2,3,8,256]{5,4,3,2,1,0:T(8,128)S(1)}, u32[]{:S(2)}, u32[]{:S(2)}) async-start(f32[64,1,2,3,8,256]{5,4,3,2,1,0:T(8,128)} %stack.19), calls=%async_computation.1 | async-start | bytes 6291456 | tf_op jit(solution)/shard_map/all_to_all | solution.py:18
  122.2 0.7 fusion.98
  122.9 1.9 collective-permute-start.2
  124.8 1.3 collective-permute-start.3
  126.1 0.6 dynamic-slice
  126.7 1.3 dynamic-slice.2
  127.9 0.5 broadcast.228.clone
  128.4 2.4 %bitcast_dynamic-update-slice_fusion.1 = f32[4]{0:T(128)} fusion(f32[4]{0:T(128)} %broadcast.228.clone, u32[]{:T(128)} %bitcast.26, f32[1,1]{1,0:T(1,128)} %dynamic-slice.2), kind=kLoop, calls=%fused_computation.138 | loop fusion | bytes 1040
  130.9 1.4 bitcast_dynamic-update-slice_fusion
  132.3 1.3 constant_dynamic-slice_fusion.5
  133.6 1.3 constant_dynamic-slice_fusion.3
  134.8 0.5 fusion.74
  135.4 8.3 %all-reduce.2 = (f32[4]{0:T(128)}, f32[4]{0:T(128)}) all-reduce(f32[4]{0:T(128)} %bitcast_dynamic-update-slice_fusion.1, f32[4]{0:T(128)S(1)} %bitcast_dynamic-update-slice_fusion), channel_id=2, replica_groups=mesh['circ'=64,'ax'=4] {'ax'}, use_global_device_ids=true, to_apply=%add | all-reduce | flops 8 | bytes 64
  143.7 0.6 constant_dynamic-update-slice_fusion.2
  144.3 1.8 fusion.11
  146.1 0.7 copy-done.3
  146.8 0.7 slice.150
  147.5 1.1 copy.17
  148.6 5.7 %all-gather.1 = f32[12,8,8,1]{2,1,3,0:T(8,128)} all-gather(f32[3,8,8,1]{2,1,3,0:T(8,128)S(1)} %copy.17), channel_id=3, replica_groups=mesh['circ'=64,'ax'=4] {'ax'}, dimensions={0}, use_global_device_ids=true | all-gather | bytes 3840 | tf_op jit(solution)/shard_map/all_gather | solution.py:39
  154.3 2.2 %fusion.9 = f32[3,8,8,256]{3,2,1,0:T(8,128)} fusion(f32[4,256,256]{2,1,0:T(8,128)} %constant.190.clone, s32[]{:T(128)S(6)} %select_n.84, f32[3,8,8,256]{3,2,1,0:T(8,128)} %copy-done.3, f32[256]{0:T(256)} %bitcast.94, f32[3,8,8]{2,1,0:T(8,128)S(1)} %get-tuple-element.131, f32[256]{0:T(256)} %bitcast.92), kind=kOutput, calls=%fused_computation.26 | convolution fusion | flops 151142400 | bytes 658180 | tf_op jit(solution)/shard_map/fnck,jk->fncj/dot_general | solution.py:244
  156.5 1.5 slice.151
  158.0 1.1 copy.18
  159.1 13.4 %all-gather.3 = f32[12,8,8,1]{2,1,3,0:T(8,128)} all-gather(f32[3,8,8,1]{2,1,3,0:T(8,128)S(1)} %copy.18), channel_id=5, replica_groups=mesh['circ'=64,'ax'=4] {'ax'}, dimensions={0}, use_global_device_ids=true | all-gather | bytes 3840 | tf_op jit(solution)/shard_map/all_gather | solution.py:39
  172.5 7.8 %while.27 = (s32[]{:T(128)}, f32[3,8,8]{2,1,0:T(8,128)S(1)}, s32[]{:T(128)}, f32[4,1,1,1]{0,3,2,1:T(1,128)}, f32[4,3,8,8]{3,2,1,0:T(8,128)}, /*index=5*/s32[]{:T(128)}, s32[]{:T(128)}, s32[]{:T(128)}, s32[]{:T(128)}) while((s32[]{:T(128)}, f32[3,8,8]{2,1,0:T(8,128)S(1)}, s32[]{:T(128)}, f32[4,1,1,1]{0,3,2,1:T(1,128)}, ...), condition=%wide.region_3.4_spmd, body=%wide.region_2.3_spmd.sunk | while | flops 390 | bytes 2471 | solution.py:48
  172.5 1.2 constant_dynamic-slice_fusion.9
  173.8 1.4 bitcast_add_fusion.5
  175.1 1.2 constant_dynamic-slice_fusion.9
  176.4 1.4 bitcast_add_fusion.5
  177.7 1.2 constant_dynamic-slice_fusion.9
  179.0 1.4 bitcast_add_fusion.5
  180.3 1.7 multiply_add_fusion.1
  182.0 12.0 %all-to-all-done.1 = f32[64,1,2,3,8,256]{5,4,3,2,1,0:T(8,128)S(1)} async-done(((f32[64,1,2,3,8,256]{5,4,3,2,1,0:T(8,128)}), f32[64,1,2,3,8,256]{5,4,3,2,1,0:T(8,128)S(1)}, u32[]{:S(2)}, u32[]{:S(2)}) %all-to-all-start.1) | async-done | bytes 3145760 | tf_op jit(solution)/shard_map/all_to_all | solution.py:18
  194.1 3.3 %fusion = f32[2,1,3,8,256]{4,1,3,2,0:T(1,128)S(1)} fusion(f32[64,2,1,1,1]{0,2,4,3,1:T(1,128)S(1)} %bitcast.90, f32[64,2,3,8,256]{4,3,2,1,0:T(8,128)S(1)} %bitcast.82), kind=kOutput, calls=%fused_computation.4 | convolution fusion | flops 9437184 | bytes 3195392 | tf_op jit(solution)/shard_map/qs,qsfna->sfna/dot_general | solution.py:208
  197.4 0.8 multiply_add_fusion
  198.2 0.8 slice_bitcast_fusion
  (31 shorter events, 0.7 us)
Async XLA Ops:
  0.6 20.1 %copy-start.5 = (f32[2,8,8,1,1]{2,1,4,3,0:T(8,128)S(1)}, f32[2,8,8,1,1]{2,1,4,3,0:T(8,128)}, u32[]{:S(2)}) copy-start(f32[2,8,8,1,1]{2,1,4,3,0:T(8,128)} %constant.206) | copy-start | bytes 1540
  1.7 6.7 %collective-permute-start = (f32[3,8,5,256]{3,2,1,0:T(8,128)S(1)}, f32[3,8,5,256]{3,2,1,0:T(8,128)S(1)}, u32[]{:S(2)}, u32[]{:S(2)}) collective-permute-start(f32[3,8,5,256]{3,2,1,0:T(8,128)S(1)} %get-tuple-element.162), channel_id=1, source_target_pairs={{4,0},{8,4},{12,8},{16,12},{20,16},{24,20},{28,24},{32,28},{36,32}... | collective-permute-start | bytes 368648 | tf_op jit(solution)/shard_map/ppermute | solution.py:30
  4.0 13.6 %collective-permute-start.1 = (f32[3,8,5,256]{3,2,1,0:T(8,128)S(1)}, f32[3,8,5,256]{3,2,1,0:T(8,128)S(1)}, u32[]{:S(2)}, u32[]{:S(2)}) collective-permute-start(f32[3,8,5,256]{3,2,1,0:T(8,128)S(1)} %get-tuple-element.163), channel_id=1, source_target_pairs={{0,4},{4,8},{8,12},{12,16},{16,20},{20,24},{24,28},{28,32},{32,36}... | collective-permute-start | bytes 368648 | tf_op jit(solution)/shard_map/ppermute | solution.py:29
  23.3 84.2 %all-to-all-start = ((f32[64,1,2,3,8,256]{5,4,3,2,1,0:T(8,128)}), f32[64,1,2,3,8,256]{5,4,3,2,1,0:T(8,128)S(1)}, u32[]{:S(2)}, u32[]{:S(2)}) async-start(f32[64,1,2,3,8,256]{5,4,3,2,1,0:T(8,128)} %stack.18), calls=%async_computation | async-start | bytes 6291456 | tf_op jit(solution)/shard_map/all_to_all | solution.py:18
  34.9 75.8 %copy-start.4 = (f32[2,8,8,1,1]{2,1,4,3,0:T(8,128)S(1)}, f32[2,8,8,1,1]{2,1,4,3,0:T(8,128)}, u32[]{:S(2)}) copy-start(f32[2,8,8,1,1]{2,1,4,3,0:T(8,128)} %constant.207) | copy-start | bytes 1540
  112.0 2.1 %copy-start.1 = (f32[2,3,8,8,256]{4,3,2,1,0:T(8,128)}, f32[2,3,8,8,256]{4,3,2,1,0:T(8,128)S(1)}, u32[]{:S(2)}) copy-start(f32[2,3,8,8,256]{4,3,2,1,0:T(8,128)S(1)} %convolution_bitcast_fusion) | copy-start | bytes 1179652
  114.1 8.1 %copy-start = (f32[3,8,8,256]{3,2,1,0:T(8,128)S(1)}, f32[3,8,8,256]{3,2,1,0:T(8,128)}, u32[]{:S(2)}) copy-start(f32[3,8,8,256]{3,2,1,0:T(8,128)} %param.16) | copy-start | bytes 589828
  114.1 12.0 %copy-start.6 = (u32[256]{0:T(256)S(1)}, u32[256]{0:T(256)}, u32[]{:S(2)}) copy-start(u32[256]{0:T(256)} %constant.196) | copy-start | bytes 3076
  114.1 80.0 %all-to-all-start.1 = ((f32[64,1,2,3,8,256]{5,4,3,2,1,0:T(8,128)}), f32[64,1,2,3,8,256]{5,4,3,2,1,0:T(8,128)S(1)}, u32[]{:S(2)}, u32[]{:S(2)}) async-start(f32[64,1,2,3,8,256]{5,4,3,2,1,0:T(8,128)} %stack.19), calls=%async_computation.1 | async-start | bytes 6291456 | tf_op jit(solution)/shard_map/all_to_all | solution.py:18
  122.9 21.4 %collective-permute-start.2 = (f32[3,8,8,2]{3,2,1,0:T(8,128)S(1)}, f32[3,8,8,2]{3,2,1,0:T(8,128)}, u32[]{:S(2)}, u32[]{:S(2)}) collective-permute-start(f32[3,8,8,2]{3,2,1,0:T(8,128)S(1)} %get-tuple-element.159), channel_id=1, source_target_pairs={{0,1},{1,2},{2,3},{4,5},{5,6},{6,7},{8,9},{9,10},{10,11},{12,13},{... | collective-permute-start | bytes 4616 | tf_op jit(solution)/shard_map/ppermute | solution.py:29
  124.8 18.9 %collective-permute-start.3 = (f32[3,8,8,2]{3,2,1,0:T(8,128)}, f32[3,8,8,2]{3,2,1,0:T(8,128)S(1)}, u32[]{:S(2)}, u32[]{:S(2)}) collective-permute-start(f32[3,8,8,2]{3,2,1,0:T(8,128)} %get-tuple-element.160), channel_id=1, source_target_pairs={{1,0},{2,1},{3,2},{5,4},{6,5},{7,6},{9,8},{10,9},{11,10},{13,12},{... | collective-permute-start | bytes 4616 | tf_op jit(solution)/shard_map/ppermute | solution.py:30
  146.1 0.7 copy-start.3
  146.8 50.6 %copy-start.2 = (f32[2,3,8,8,256]{4,3,2,1,0:T(8,128)S(1)}, f32[2,3,8,8,256]{4,3,2,1,0:T(8,128)}, u32[]{:S(2)}) copy-start(f32[2,3,8,8,256]{4,3,2,1,0:T(8,128)} %copy-done.1) | copy-start | bytes 1179652
